TPU v7x, 256 devices: a whole 4x4x8 slice. The times are simulated.
256 devices in a mesh: dp: 64 (over y, z_hi, x), mp: 4 (over z_lo, core).
Axes of the slice: x: 4, y: 4, z: 8 (z_hi: 4, z_lo: 2; z = z_hi * 2 + z_lo), core: 2. Of those that a mesh axis runs over, the one named last changes fastest.
Arguments:
- tokens: bfloat16 [4096, 2, 3072], P('dp'), may hold values from -6 to 6
- norm_gain_vector: float32 [3072], replicated, may hold values from 0.5 to 1.5
- query_weight: bfloat16 [3072, 1536], P('dp', 'mp'), may hold values from -0.109375 to 0.109375
- key_weight: bfloat16 [3072, 1536], P('dp', 'mp'), may hold values from -0.4375 to 0.4375
- value_weight: bfloat16 [3072, 1536], P('dp', 'mp'), may hold values from -0.109375 to 0.109375
- output_weight: bfloat16 [3072, 1536], P('dp', 'mp'), may hold values from -0.15625 to 0.15625
- prefix_cache: bfloat16 [64, 64, 2, 1536], P('dp', None, None, 'mp'), may hold values from -64 to 64
- lengths: int32 [4096], P('dp'), may hold values from 1 to 2, 5120 in all
- groups: int32 [4096], P('dp'), may hold values from 0 to 3
- deal_slot: int32 [4096], P('dp'), may hold values from 0 to 4095, as said below
- owners: int32 [64], replicated, may hold values from 0 to 63, each once
Outputs:
- hidden: bfloat16 [4096, 2, 3072], P('dp', None, 'mp')
- suffix_cache: bfloat16 [4096, 2, 2, 1536], P('dp', None, None, 'mp')
Inputs may be any that keep to these rules, and one draw needn't show every extreme that they name: Every value once; the 64 requests that start on one index of dp go to 64 different devices deal_slot // 64, one to each.
All inputs are finite; a program needn't handle non-finite values. No bound on the sum of `lengths` on one device may be relied on, other than what follows from the above.
Results may differ from a plain program's by a relative error of at most 0.013.
The roundings to bfloat16 on the way count: a program that leaves them out, or rounds other values in their place, can miss the bound.
Values may be sent and summed in bfloat16 or wider, within the bound.
No kernel may reach another device: no remote copies, remote signals or barrier semaphores. Data moves between devices by JAX's collectives and lax.ppermute only.
A program may use at most 128 MiB of HBM per device.

v0:
```python
import math
import jax
import jax.numpy as jnp
from jax import lax
from jax.sharding import PartitionSpec as P

HD = 96
GROUPS = 4
PBLK = 64
NEG_FILL = -1e30


def rope_tables(slot_len, head_dim, first_pos):
    position = (first_pos + jnp.arange(slot_len)).astype(jnp.float32)
    frequency = 10000.0 ** (-jnp.arange(head_dim // 2).astype(jnp.float32) * 2.0 / head_dim)
    angles = position[:, None] * frequency[None, :]
    angles = jnp.concatenate([angles, angles], axis=-1)
    return (jnp.cos(angles)[:, None, :], jnp.sin(angles)[:, None, :])


def rope_rotate(values, cosine, sine_table):
    half_dim = values.shape[-1] // 2
    turned = jnp.concatenate([-values[..., half_dim:], values[..., :half_dim]], axis=-1)
    return values * cosine + turned * sine_table


def project(tokens, norm_gain_vector, query_weight, key_weight, value_weight, prefix_len):
    requests, slot_len, model_width = tokens.shape
    widened_rows = tokens.astype(jnp.float32)
    reciprocal_root_scale = lax.rsqrt(
        jnp.mean(widened_rows * widened_rows, axis=-1, keepdims=True) + 1e-05
    )
    normalized_rows = (
        (widened_rows * reciprocal_root_scale * norm_gain_vector)
        .astype(jnp.bfloat16)
        .reshape(requests * slot_len, model_width)
    )
    head_cols = query_weight.shape[1]
    pieces = (
        lax.all_gather(query_weight, "dp", axis=0, tiled=True),
        lax.all_gather(key_weight, "dp", axis=0, tiled=True),
        lax.all_gather(value_weight, "dp", axis=0, tiled=True),
    )
    queries, keyed, valued = tuple(
        (
            jnp.dot(normalized_rows, weight_rows, preferred_element_type=jnp.float32)
            for weight_rows in pieces
        )
    )
    heads_local = head_cols // HD
    cosine, sine_table = rope_tables(slot_len, HD, prefix_len)

    def shaped(values):
        return values.reshape(requests, slot_len, heads_local, HD)

    queries = (
        rope_rotate(shaped(queries), cosine, sine_table)
        .astype(jnp.bfloat16)
        .reshape(requests, slot_len, head_cols)
    )
    keyed = (
        rope_rotate(shaped(keyed), cosine, sine_table)
        .astype(jnp.bfloat16)
        .reshape(requests, slot_len, head_cols)
    )
    valued = valued.astype(jnp.bfloat16).reshape(requests, slot_len, head_cols)
    return jnp.concatenate([queries, keyed, valued], axis=-1)


def attend(packed, length_in, group_in, prefix_cache, owners):
    requests, slot_len, triple = packed.shape
    head_cols = triple // 3
    heads_local = head_cols // HD
    row_count = requests * slot_len
    devices = lax.axis_size("dp")
    blocks_per = devices // GROUPS
    inv_scale = 1.0 / math.sqrt(HD)
    queries = packed[..., :head_cols].reshape(requests, slot_len, heads_local, HD)
    keyed = packed[..., head_cols : 2 * head_cols].reshape(requests, slot_len, heads_local, HD)
    valued = packed[..., 2 * head_cols :].reshape(requests, slot_len, heads_local, HD)
    position = jnp.arange(slot_len)
    allowed = (position[None, :, None] >= position[None, None, :]) & (
        position[None, None, :] < length_in[:, None, None]
    )
    allowed = allowed[:, None]
    self_scores = (
        jnp.einsum("rthd,rshd->rhts", queries, keyed, preferred_element_type=jnp.float32)
        * inv_scale
    )
    self_max = jnp.max(jnp.where(allowed, self_scores, NEG_FILL), axis=-1)
    self_weights = jnp.where(allowed, jnp.exp(self_scores - self_max[..., None]), 0.0)
    self_sum = jnp.sum(self_weights, axis=-1)
    self_acc = jnp.einsum(
        "rhts,rshd->rhtd",
        self_weights.astype(jnp.bfloat16),
        valued,
        preferred_element_type=jnp.float32,
    )
    run_max = jnp.transpose(self_max, (1, 0, 2)).reshape(heads_local, row_count)
    run_sum = jnp.transpose(self_sum, (1, 0, 2)).reshape(heads_local, row_count)
    run_acc = jnp.transpose(self_acc, (1, 0, 2, 3)).reshape(heads_local, row_count, HD)
    flat_queries = queries.reshape(row_count, heads_local, HD)
    query_group = jnp.repeat(group_in, slot_len)
    slot_ids = jnp.arange(devices, dtype=jnp.int32)
    owner_match = owners[None, :] == slot_ids[:, None]
    slot_group = jnp.sum(jnp.where(owner_match, (slot_ids // blocks_per)[None, :], 0), axis=1)
    shard_rows = lax.all_gather(prefix_cache, "dp", axis=0, tiled=True)
    slot_count = shard_rows.shape[0]
    block_len = shard_rows.shape[1]
    key_count = slot_count * block_len
    key_rows = shard_rows[:, :, 0].reshape(key_count, heads_local, HD)
    value_rows = shard_rows[:, :, 1].reshape(key_count, heads_local, HD)
    key_slot = jnp.arange(key_count, dtype=jnp.int32) // block_len
    key_group = jnp.sum(
        jnp.where(key_slot[:, None] == slot_ids[None, :], slot_group[None, :], 0), axis=1
    )
    key_block = math.gcd(key_count, 512)

    def absorb_block(carry_state, block_index):
        prior_max, prior_sum, prior_acc = carry_state
        keys_of_block = lax.dynamic_slice_in_dim(key_rows, block_index * key_block, key_block, 0)
        block_values = lax.dynamic_slice_in_dim(value_rows, block_index * key_block, key_block, 0)
        block_group = lax.dynamic_slice_in_dim(key_group, block_index * key_block, key_block, 0)
        scores = (
            jnp.einsum(
                "qhd,khd->hqk", flat_queries, keys_of_block, preferred_element_type=jnp.float32
            )
            * inv_scale
        )
        matched = (query_group[:, None] == block_group[None, :])[None]
        block_max = jnp.max(jnp.where(matched, scores, NEG_FILL), axis=-1)
        new_max = jnp.maximum(prior_max, block_max)
        weights = jnp.where(matched, jnp.exp(scores - new_max[..., None]), 0.0)
        shrink = jnp.exp(prior_max - new_max)
        new_sum = prior_sum * shrink + jnp.sum(weights, axis=-1)
        new_acc = prior_acc * shrink[..., None] + jnp.einsum(
            "hqk,khd->hqd",
            weights.astype(jnp.bfloat16),
            block_values,
            preferred_element_type=jnp.float32,
        )
        return ((new_max, new_sum, new_acc), None)

    carry_out, _ = lax.scan(
        absorb_block, (run_max, run_sum, run_acc), jnp.arange(key_count // key_block)
    )
    run_max, run_sum, run_acc = carry_out
    attended = (run_acc / run_sum[..., None]).astype(jnp.bfloat16)
    attended = jnp.transpose(attended, (1, 0, 2)).reshape(requests, slot_len, head_cols)
    live_mask = position[None, :] < length_in[:, None]
    stacked_parts = jnp.stack(
        [packed[..., head_cols : 2 * head_cols], packed[..., 2 * head_cols :]], axis=2
    )
    stacked_parts = jnp.where(
        live_mask[:, :, None, None], stacked_parts, jnp.zeros_like(stacked_parts)
    )
    return (attended, stacked_parts)


def on_device(
    tokens,
    norm_gain_vector,
    query_weight,
    key_weight,
    value_weight,
    output_weight,
    prefix_cache,
    lengths,
    groups,
    deal_slot,
    owners,
):
    requests, slot_len, model_width = tokens.shape
    devices = lax.axis_size("dp")
    head_cols = query_weight.shape[1]
    prefix_len = PBLK * devices // GROUPS
    dest_device = deal_slot // requests
    send_order = jnp.argsort(dest_device)
    restore = jnp.argsort(send_order)
    request_info = jnp.stack([deal_slot, lengths, groups], axis=1)
    moved_rows, info_in = (
        lax.all_to_all(tokens[send_order], "dp", split_axis=0, concat_axis=0, tiled=True),
        lax.all_to_all(request_info[send_order], "dp", split_axis=0, concat_axis=0, tiled=True),
    )
    packed = project(
        moved_rows, norm_gain_vector, query_weight, key_weight, value_weight, prefix_len
    )
    attended, stacked_parts = attend(packed, info_in[:, 1], info_in[:, 2], prefix_cache, owners)
    suffix_cache = stacked_parts[jnp.argsort(info_in[:, 0] % requests)]
    attended_home = lax.all_to_all(attended, "dp", split_axis=0, concat_axis=0, tiled=True)[restore]
    flat_attended = attended_home.reshape(requests * slot_len, head_cols)
    partial_terms = lax.dot_general(
        flat_attended,
        lax.all_gather(output_weight, "dp", axis=0, tiled=True),
        (((1,), (1,)), ((), ())),
        preferred_element_type=jnp.float32,
    )
    summed = lax.psum_scatter(
        partial_terms.astype(jnp.bfloat16), "mp", scatter_dimension=1, tiled=True
    ).astype(jnp.float32)
    live_mask = (jnp.arange(slot_len)[None, :] < lengths[:, None]).reshape(requests * slot_len, 1)
    hidden = (
        jnp.where(live_mask, summed, 0.0)
        .astype(jnp.bfloat16)
        .reshape(requests, slot_len, summed.shape[1])
    )
    return (hidden, suffix_cache)


def solution(mesh):
    in_specs = (
        P("dp", None, None),
        P(),
        P("dp", "mp"),
        P("dp", "mp"),
        P("dp", "mp"),
        P("dp", "mp"),
        P("dp", None, None, "mp"),
        P("dp"),
        P("dp"),
        P("dp"),
        P(),
    )
    out_specs = (P("dp", None, "mp"), P("dp", None, None, "mp"))
    return jax.shard_map(
        on_device, mesh=mesh, in_specs=in_specs, out_specs=out_specs, check_vma=False
    )
```

profile of v0, /device:TPU:1, one launch (start us, length us, event | category | flops | bytes accessed | tf_op | source)
XLA Modules:
  0.0 492.5 jit_solution(8548728937993800416)
XLA Ops:
  15.7 15.1 %all-to-all-start = ((s32[64,1,3]{2,1,0:T(1,128)}), s32[64,1,3]{2,1,0:T(1,128)S(1)}, u32[]{:S(2)}, u32[]{:S(2)}) async-start(s32[64,1,3]{2,1,0:T(1,128)} %bitcast.4), calls=%async_computation | async-start | bytes 65536 | tf_op jit(solution)/shard_map/all_to_all | solution.py:183
  31.5 3.0 gather_fusion.1
  34.5 2.1 sort.46
  36.6 5.1 %all-to-all-done = s32[64,1,3]{2,1,0:T(1,128)S(1)} async-done(((s32[64,1,3]{2,1,0:T(1,128)}), s32[64,1,3]{2,1,0:T(1,128)S(1)}, u32[]{:S(2)}, u32[]{:S(2)}) %all-to-all-start) | async-done | bytes 800 | tf_op jit(solution)/shard_map/all_to_all | solution.py:183
  41.6 7.3 %all-to-all-start.1 = ((bf16[64,2,3072]{2,1,0:T(2,128)(2,1)}), bf16[64,2,3072]{2,1,0:T(2,128)(2,1)S(1)}, u32[]{:S(2)}, u32[]{:S(2)}) async-start(bf16[64,2,3072]{2,1,0:T(2,128)(2,1)} %gather_fusion.1), calls=%async_computation.1 | async-start | bytes 1572864 | tf_op jit(solution)/shard_map/all_to_all | solution.py:182
  50.0 22.7 %all-to-all-done.1 = bf16[64,2,3072]{2,1,0:T(2,128)(2,1)S(1)} async-done(((bf16[64,2,3072]{2,1,0:T(2,128)(2,1)}), bf16[64,2,3072]{2,1,0:T(2,128)(2,1)S(1)}, u32[]{:S(2)}, u32[]{:S(2)}) %all-to-all-start.1) | async-done | bytes 786464 | tf_op jit(solution)/shard_map/all_to_all | solution.py:182
  75.8 22.8 %all-gather.6.cloned.1.call-done = bf16[3072,384]{1,0:T(8,128)(2,1)} async-done(((bf16[48,384]{1,0:T(8,128)(2,1)}), bf16[3072,384]{1,0:T(8,128)(2,1)}) %all-gather.6.cloned.1.call-update) | async-done | bytes 2359312 | tf_op jit(solution)/shard_map/all_gather | solution.py:40
  98.7 4.3 copy.143
  102.9 76.2 %all-gather.8.cloned.1.call-done = bf16[3072,384]{1,0:T(8,128)(2,1)} async-done(((bf16[48,384]{1,0:T(8,128)(2,1)}), bf16[3072,384]{1,0:T(8,128)(2,1)}) %all-gather.8.cloned.1.call-update) | async-done | bytes 2359312 | tf_op jit(solution)/shard_map/all_gather | solution.py:41
  179.2 4.3 copy.145
  183.5 2.9 fusion.19
  188.8 70.9 %all-gather.10.cloned.1.call-done = bf16[3072,384]{1,0:T(8,128)(2,1)} async-done(((bf16[48,384]{1,0:T(8,128)(2,1)}), bf16[3072,384]{1,0:T(8,128)(2,1)}) %all-gather.10.cloned.1.call-update) | async-done | bytes 2359312 | tf_op jit(solution)/shard_map/all_gather | solution.py:42
  259.7 2.2 convolution_convert_fusion.1
  263.2 98.9 %all-gather.12.cloned.1.call-done = bf16[64,64,2,384]{3,1,2,0:T(8,128)(2,1)} async-done(((bf16[1,64,2,384]{3,1,2,0:T(8,128)(2,1)}), bf16[64,64,2,384]{3,1,2,0:T(8,128)(2,1)}) %all-gather.12.cloned.1.call-update) | async-done | bytes 6291472 | tf_op jit(solution)/shard_map/all_gather | solution.py:107
  362.1 6.2 %fusion.38 = (bf16[64,64,1,384]{3,1,2,0:T(8,128)(2,1)}, bf16[64,64,1,384]{3,1,2,0:T(8,128)(2,1)}) fusion(bf16[64,64,2,384]{3,1,2,0:T(8,128)(2,1)} %all-gather.12.cloned.1.call-done), kind=kLoop, calls=%fused_computation.99 | loop fusion | bytes 12582912 | tf_op jit(solution)/shard_map/slice | solution.py:112
  368.4 8.8 %reshape_squeeze.6 = bf16[4096,4,96]{2,1,0:T(4,128)(2,1)} reshape(bf16[64,64,1,384]{3,1,2,0:T(8,128)(2,1)} %get-tuple-element.164) | data formatting | bytes 6291456 | tf_op jit(solution)/shard_map/reshape;squeeze | solution.py:111
  377.2 7.3 %copy.163 = bf16[4096,4,96]{0,2,1:T(8,128)(2,1)} copy(bf16[4096,4,96]{2,1,0:T(4,128)(2,1)} %reshape_squeeze.6) | data formatting | bytes 6291456
  384.5 8.8 %reshape_squeeze.7 = bf16[4096,4,96]{2,1,0:T(4,128)(2,1)} reshape(bf16[64,64,1,384]{3,1,2,0:T(8,128)(2,1)} %get-tuple-element.163) | data formatting | bytes 6291456 | tf_op jit(solution)/shard_map/reshape;squeeze | solution.py:112
  393.3 7.3 %copy.165 = bf16[4096,4,96]{0,2,1:T(8,128)(2,1)} copy(bf16[4096,4,96]{2,1,0:T(4,128)(2,1)} %reshape_squeeze.7) | data formatting | bytes 6291456
  400.6 37.5 %while.15 = (s32[]{:T(128)}, f32[4,128]{1,0:T(4,128)S(1)}, f32[4,128]{1,0:T(4,128)S(1)}, f32[4,128,96]{1,2,0:T(8,128)S(1)}, s32[8]{0:T(128)S(1)}, /*index=5*/s32...) while((s32[]{:T(128)}, f32[4,128]{1,0:T(4,128)S(1)}, ...), condition=%wide.region_9.10_spmd.clone, body=%wide.region_6.9_spmd.clone.sunk | while | flops 103187456 | bytes 4727243 | solution.py:144
  439.2 11.7 %all-to-all-start.2 = ((bf16[64,2,384]{2,1,0:T(2,128)(2,1)}), bf16[64,2,384]{2,1,0:T(2,128)(2,1)S(1)}, u32[]{:S(2)}, u32[]{:S(2)}) async-start(bf16[64,2,384]{2,1,0:T(2,128)(2,1)} %reshape.253), calls=%async_computation.2 | async-start | bytes 196608 | tf_op jit(solution)/shard_map/all_to_all | solution.py:190
  451.1 11.1 %all-to-all-done.2 = bf16[64,2,384]{2,1,0:T(2,128)(2,1)S(1)} async-done(((bf16[64,2,384]{2,1,0:T(2,128)(2,1)}), bf16[64,2,384]{2,1,0:T(2,128)(2,1)S(1)}, u32[]{:S(2)}, u32[]{:S(2)}) %all-to-all-start.2) | async-done | bytes 98336 | tf_op jit(solution)/shard_map/all_to_all | solution.py:190
  463.1 3.4 convolution_convert_fusion
  471.4 12.5 %reduce-scatter.2.cloned.1.call-done = bf16[128,768]{1,0:T(8,128)(2,1)} async-done(((bf16[128,3072]{1,0:T(8,128)(2,1)}), bf16[128,768]{1,0:T(8,128)(2,1)}) %reduce-scatter.2.cloned.1.call-update) | async-done | bytes 196624 | tf_op jit(solution)/shard_map/reduce_scatter | solution.py:198
  (179 shorter events, 57.3 us)
Async XLA Ops:
  7.2 24.3 %copy-start = (bf16[64,2,3072]{2,1,0:T(2,128)(2,1)S(1)}, bf16[64,2,3072]{2,1,0:T(2,128)(2,1)}, u32[]{:S(2)}) copy-start(bf16[64,2,3072]{2,1,0:T(2,128)(2,1)} %param.13) | copy-start | bytes 2359300
  7.2 42.0 %copy-start.4 = (s32[64]{0:T(128)S(1)}, s32[64]{0:T(128)}, u32[]{:S(2)}) copy-start(s32[64]{0:T(128)} %param.23) | copy-start | bytes 772
  7.2 91.5 %all-gather.6.cloned.1.call-start = ((), (), s32[]{:S(2)}) async-start(), calls=%async_computation.4 | async-start | bytes 2396160 | tf_op jit(solution)/shard_map/all_gather | solution.py:40
  7.9 171.3 %all-gather.8.cloned.1.call-start = ((), (), s32[]{:S(2)}) async-start(), calls=%async_computation.5 | async-start | bytes 2396160 | tf_op jit(solution)/shard_map/all_gather | solution.py:41
  8.7 251.0 %all-gather.10.cloned.1.call-start = ((), (), s32[]{:S(2)}) async-start(), calls=%async_computation.6 | async-start | bytes 2396160 | tf_op jit(solution)/shard_map/all_gather | solution.py:42
  9.4 352.7 %all-gather.12.cloned.1.call-start = ((), (), s32[]{:S(2)}) async-start(), calls=%async_computation.7 | async-start | bytes 6389760 | tf_op jit(solution)/shard_map/all_gather | solution.py:107
  11.0 62.6 %copy-start.2 = (f32[3072]{0:T(1024)S(1)}, f32[3072]{0:T(1024)}, u32[]{:S(2)}) copy-start(f32[3072]{0:T(1024)} %param.14) | copy-start | bytes 36868
  15.7 25.9 %all-to-all-start = ((s32[64,1,3]{2,1,0:T(1,128)}), s32[64,1,3]{2,1,0:T(1,128)S(1)}, u32[]{:S(2)}, u32[]{:S(2)}) async-start(s32[64,1,3]{2,1,0:T(1,128)} %bitcast.4), calls=%async_computation | async-start | bytes 65536 | tf_op jit(solution)/shard_map/all_to_all | solution.py:183
  30.9 432.2 %all-gather.14.cloned.1.call-start = ((), (), s32[]{:S(2)}) async-start(), calls=%async_computation.8 | async-start | bytes 2396160 | tf_op jit(solution)/shard_map/all_gather | solution.py:194
  41.6 31.1 %all-to-all-start.1 = ((bf16[64,2,3072]{2,1,0:T(2,128)(2,1)}), bf16[64,2,3072]{2,1,0:T(2,128)(2,1)S(1)}, u32[]{:S(2)}, u32[]{:S(2)}) async-start(bf16[64,2,3072]{2,1,0:T(2,128)(2,1)} %gather_fusion.1), calls=%async_computation.1 | async-start | bytes 1572864 | tf_op jit(solution)/shard_map/all_to_all | solution.py:182
  183.5 2.9 copy-start.1
  439.2 27.3 %copy-start.3 = (s32[64]{0:T(128)S(1)}, s32[64]{0:T(128)}, u32[]{:S(2)}) copy-start(s32[64]{0:T(128)} %param.20) | copy-start | bytes 772
  439.2 23.0 %all-to-all-start.2 = ((bf16[64,2,384]{2,1,0:T(2,128)(2,1)}), bf16[64,2,384]{2,1,0:T(2,128)(2,1)S(1)}, u32[]{:S(2)}, u32[]{:S(2)}) async-start(bf16[64,2,384]{2,1,0:T(2,128)(2,1)} %reshape.253), calls=%async_computation.2 | async-start | bytes 196608 | tf_op jit(solution)/shard_map/all_to_all | solution.py:190
  451.0 32.9 %reduce-scatter.2.cloned.1.call-start = ((), (), s32[]{:S(2)}) async-start(), calls=%async_computation.9 | async-start | bytes 983040 | tf_op jit(solution)/shard_map/reduce_scatter | solution.py:198
Sparse Core Ops, SparseCore 0:
  11.2 87.4 all-gather.5
  101.8 77.2 all-gather.7
  182.4 77.2 all-gather.9
  263.4 98.6 all-gather.11
  365.2 77.9 all-gather.13
  466.6 17.2 reduce-scatter.1
where the time goes:
time: 494 us; the launch traced here: 493 us
  waiting for transfers between devices  323 us (65%)
  local copies, waits for them, and re-layouts  66.6 us (13%)
  starting transfers between devices  34.4 us (7%)
  matrix products  32.3 us (7%)
  other arithmetic  16.1 us (3%)
  between operations  14.5 us (3%)
  loops' own time  5.66 us (1%)
    all_gather x1, waiting for transfers between devices, attend(): shard_rows = lax.all_gather(prefix_cache, 'dp', axis=0, tiled=True)  98.9 us
    all_gather x1, waiting for transfers between devices, project(): lax.all_gather(key_weight, 'dp', axis=0, tiled=True)  76.2 us
    all_gather x1, waiting for transfers between devices, project(): lax.all_gather(value_weight, 'dp', axis=0, tiled=True)  70.9 us
    all_gather x1, waiting for transfers between devices, project(): lax.all_gather(query_weight, 'dp', axis=0, tiled=True)  22.8 us
    all_to_all x1, waiting for transfers between devices, on_device(): lax.all_to_all(tokens[send_order], 'dp', split_axis=0, concat_axis=0, til...  22.7 us
    unnamed x17, local copies, waits for them, and re-layouts  16.5 us
    all_to_all x1, starting transfers between devices, on_device(): lax.all_to_all(request_info[send_order], 'dp', split_axis=0, concat_axis=...  15.1 us
    reduce_scatter x1, waiting for transfers between devices, on_device(): lax.psum_scatter(partial_terms.astype(jnp.bfloat16), 'mp', scatter_dimens...  12.5 us
  transfers between devices with their start and end apart: 9, of which 8 were waited for; matrix products, arithmetic and copies ran while one was open for 22% of the time, Pallas kernels for 0%

commit v1 on v0

--- a/solution.py
+++ b/solution.py
@@ -104,7 +104,9 @@
     slot_ids = jnp.arange(devices, dtype=jnp.int32)
     owner_match = owners[None, :] == slot_ids[:, None]
     slot_group = jnp.sum(jnp.where(owner_match, (slot_ids // blocks_per)[None, :], 0), axis=1)
-    shard_rows = lax.all_gather(prefix_cache, "dp", axis=0, tiled=True)
+    shard_rows = jnp.concatenate(
+        lax.all_to_all(jnp.stack([prefix_cache] * lax.axis_size("dp")), "dp", 0, 0), axis=0
+    )
     slot_count = shard_rows.shape[0]
     block_len = shard_rows.shape[1]
     key_count = slot_count * block_len

time: 494 us -> 476 us (0.964)
  waiting for transfers between devices: 323 us -> 297 us
  starting transfers between devices: 34.4 us -> 39.5 us
    all_gather x1 -> x0, waiting for transfers between devices: 98.9 us -> none  [attend(): shard_rows = lax.all_gather(prefix_cache, 'dp', axis=0, tiled=True)]
    all_gather x1, waiting for transfers between devices: 76.2 us -> 135 us  [project(): lax.all_gather(key_weight, 'dp', axis=0, tiled=True)]
    all_gather x1, waiting for transfers between devices: 22.8 us -> 33.4 us  [project(): lax.all_gather(query_weight, 'dp', axis=0, tiled=True)]
    all_to_all x0 -> x1, starting transfers between devices: none -> 9.75 us  [attend(): lax.all_to_all(jnp.stack([prefix_cache] * lax.axis_size('dp')), 'dp', 0, 0)]
    unnamed x17 -> x18, local copies, waits for them, and re-layouts: 16.5 us -> 14.9 us
  transfers between devices with their start and end apart: 9 -> 9, of which waited for: 8 -> 7; matrix products, arithmetic and copies ran while one was open for 22% -> 24% of each run, Pallas kernels for 0% -> 0%
where the time goes in v1:
time: 476 us; the launch traced here: 474 us
  waiting for transfers between devices  297 us (62%)
  local copies, waits for them, and re-layouts  68.6 us (14%)
  starting transfers between devices  39.5 us (8%)
  matrix products  32.4 us (7%)
  other arithmetic  16.1 us (3%)
  between operations  14.2 us (3%)
  loops' own time  5.67 us (1%)
    all_gather x1, waiting for transfers between devices, project(): lax.all_gather(key_weight, 'dp', axis=0, tiled=True)  135 us
    all_gather x1, waiting for transfers between devices, project(): lax.all_gather(value_weight, 'dp', axis=0, tiled=True)  70.9 us
    all_gather x1, waiting for transfers between devices, project(): lax.all_gather(query_weight, 'dp', axis=0, tiled=True)  33.4 us
    all_to_all x1, waiting for transfers between devices, on_device(): lax.all_to_all(tokens[send_order], 'dp', split_axis=0, concat_axis=0, til...  22.9 us
    all_to_all x1, starting transfers between devices, on_device(): lax.all_to_all(request_info[send_order], 'dp', split_axis=0, concat_axis=...  15.1 us
    unnamed x18, local copies, waits for them, and re-layouts  14.9 us
    reduce_scatter x1, waiting for transfers between devices, on_device(): lax.psum_scatter(partial_terms.astype(jnp.bfloat16), 'mp', scatter_dimens...  14.1 us
    dot_general x8, matrix products, absorb_block(): jnp.einsum('qhd,khd->hqk', flat_queries, keys_of_block, preferred_element...  11.1 us
  transfers between devices with their start and end apart: 9, of which 7 were waited for; matrix products, arithmetic and copies ran while one was open for 24% of the time, Pallas kernels for 0%

profile of v1, /device:TPU:1, one launch (start us, length us, event | category | flops | bytes accessed | tf_op | source)
XLA Modules:
  0.0 473.8 jit_solution(16097703909207399091)
XLA Ops:
  13.4 15.1 %all-to-all-start = ((s32[64,1,3]{2,1,0:T(1,128)}), s32[64,1,3]{2,1,0:T(1,128)S(1)}, u32[]{:S(2)}, u32[]{:S(2)}) async-start(s32[64,1,3]{2,1,0:T(1,128)} %bitcast.4), calls=%async_computation | async-start | bytes 65536 | tf_op jit(solution)/shard_map/all_to_all | solution.py:185
  28.5 3.0 gather_fusion.1
  31.5 7.8 %all-to-all-done = s32[64,1,3]{2,1,0:T(1,128)S(1)} async-done(((s32[64,1,3]{2,1,0:T(1,128)}), s32[64,1,3]{2,1,0:T(1,128)S(1)}, u32[]{:S(2)}, u32[]{:S(2)}) %all-to-all-start) | async-done | bytes 800 | tf_op jit(solution)/shard_map/all_to_all | solution.py:185
  39.2 4.6 all-to-all-start.1
  43.9 22.9 %all-to-all-done.1 = bf16[64,2,3072]{2,1,0:T(2,128)(2,1)S(1)} async-done(((bf16[64,2,3072]{2,1,0:T(2,128)(2,1)}), bf16[64,2,3072]{2,1,0:T(2,128)(2,1)S(1)}, u32[]{:S(2)}, u32[]{:S(2)}) %all-to-all-start.1) | async-done | bytes 786464 | tf_op jit(solution)/shard_map/all_to_all | solution.py:184
  66.8 3.7 stack.13
  70.5 9.7 %all-to-all-start.2 = ((bf16[64,1,64,2,384]{4,2,3,1,0:T(8,128)(2,1)}), bf16[64,1,64,2,384]{4,2,3,1,0:T(8,128)(2,1)}, u32[]{:S(2)}, u32[]{:S(2)}) async-start(bf16[64,1,64,2,384]{4,2,3,1,0:T(8,128)(2,1)} %stack.13), calls=%async_computation.2 | async-start | bytes 12582912 | tf_op jit(solution)/shard_map/all_to_all | solution.py:108
  87.8 33.4 %all-gather.5.cloned.1.call-done = bf16[3072,384]{1,0:T(8,128)(2,1)} async-done(((bf16[48,384]{1,0:T(8,128)(2,1)}), bf16[3072,384]{1,0:T(8,128)(2,1)}) %all-gather.5.cloned.1.call-update) | async-done | bytes 2359312 | tf_op jit(solution)/shard_map/all_gather | solution.py:40
  121.2 4.3 copy.143
  125.5 134.7 %all-gather.7.cloned.1.call-done = bf16[3072,384]{1,0:T(8,128)(2,1)} async-done(((bf16[48,384]{1,0:T(8,128)(2,1)}), bf16[3072,384]{1,0:T(8,128)(2,1)}) %all-gather.7.cloned.1.call-update) | async-done | bytes 2359312 | tf_op jit(solution)/shard_map/all_gather | solution.py:41
  260.2 4.3 copy.145
  264.5 2.9 fusion.19
  269.9 70.9 %all-gather.9.cloned.1.call-done = bf16[3072,384]{1,0:T(8,128)(2,1)} async-done(((bf16[48,384]{1,0:T(8,128)(2,1)}), bf16[3072,384]{1,0:T(8,128)(2,1)}) %all-gather.9.cloned.1.call-update) | async-done | bytes 2359312 | tf_op jit(solution)/shard_map/all_gather | solution.py:42
  340.8 2.2 convolution_convert_fusion.1
  344.3 6.2 %fusion.38 = (bf16[64,64,1,384]{3,1,2,0:T(8,128)(2,1)}, bf16[64,64,1,384]{3,1,2,0:T(8,128)(2,1)}) fusion(bf16[64,64,2,384]{3,1,2,0:T(8,128)(2,1)} %bitcast.21), kind=kLoop, calls=%fused_computation.99 | loop fusion | bytes 12582912 | tf_op jit(solution)/shard_map/slice | solution.py:114
  350.5 8.8 %reshape_squeeze.6 = bf16[4096,4,96]{2,1,0:T(4,128)(2,1)} reshape(bf16[64,64,1,384]{3,1,2,0:T(8,128)(2,1)} %get-tuple-element.164) | data formatting | bytes 6291456 | tf_op jit(solution)/shard_map/reshape;squeeze | solution.py:113
  359.4 7.2 %copy.163 = bf16[4096,4,96]{0,2,1:T(8,128)(2,1)} copy(bf16[4096,4,96]{2,1,0:T(4,128)(2,1)} %reshape_squeeze.6) | data formatting | bytes 6291456
  366.6 8.8 %reshape_squeeze.7 = bf16[4096,4,96]{2,1,0:T(4,128)(2,1)} reshape(bf16[64,64,1,384]{3,1,2,0:T(8,128)(2,1)} %get-tuple-element.163) | data formatting | bytes 6291456 | tf_op jit(solution)/shard_map/reshape;squeeze | solution.py:114
  375.4 7.3 %copy.165 = bf16[4096,4,96]{0,2,1:T(8,128)(2,1)} copy(bf16[4096,4,96]{2,1,0:T(4,128)(2,1)} %reshape_squeeze.7) | data formatting | bytes 6291456
  382.7 37.6 %while.15 = (s32[]{:T(128)}, f32[4,128]{1,0:T(4,128)S(1)}, f32[4,128]{1,0:T(4,128)S(1)}, f32[4,128,96]{1,2,0:T(8,128)S(1)}, s32[8]{0:T(128)S(1)}, /*index=5*/s32...) while((s32[]{:T(128)}, f32[4,128]{1,0:T(4,128)S(1)}, ...), condition=%wide.region_9.10_spmd.clone, body=%wide.region_6.9_spmd.clone.sunk | while | flops 103187456 | bytes 4727243 | solution.py:146
  421.4 9.6 %all-to-all-start.3 = ((bf16[64,2,384]{2,1,0:T(2,128)(2,1)}), bf16[64,2,384]{2,1,0:T(2,128)(2,1)S(1)}, u32[]{:S(2)}, u32[]{:S(2)}) async-start(bf16[64,2,384]{2,1,0:T(2,128)(2,1)} %reshape.260), calls=%async_computation.3 | async-start | bytes 196608 | tf_op jit(solution)/shard_map/all_to_all | solution.py:192
  431.3 10.9 %all-to-all-done.3 = bf16[64,2,384]{2,1,0:T(2,128)(2,1)S(1)} async-done(((bf16[64,2,384]{2,1,0:T(2,128)(2,1)}), bf16[64,2,384]{2,1,0:T(2,128)(2,1)S(1)}, u32[]{:S(2)}, u32[]{:S(2)}) %all-to-all-start.3) | async-done | bytes 98336 | tf_op jit(solution)/shard_map/all_to_all | solution.py:192
  443.1 3.4 convolution_convert_fusion
  451.3 14.1 %reduce-scatter.2.cloned.1.call-done = bf16[128,768]{1,0:T(8,128)(2,1)} async-done(((bf16[128,3072]{1,0:T(8,128)(2,1)}), bf16[128,768]{1,0:T(8,128)(2,1)}) %reduce-scatter.2.cloned.1.call-update) | async-done | bytes 196624 | tf_op jit(solution)/shard_map/reduce_scatter | solution.py:200
  (181 shorter events, 58.0 us)
Async XLA Ops:
  7.2 21.3 %copy-start = (bf16[64,2,3072]{2,1,0:T(2,128)(2,1)S(1)}, bf16[64,2,3072]{2,1,0:T(2,128)(2,1)}, u32[]{:S(2)}) copy-start(bf16[64,2,3072]{2,1,0:T(2,128)(2,1)} %param.13) | copy-start | bytes 2359300
  7.2 36.7 %copy-start.2 = (bf16[1,64,2,384]{3,2,1,0:T(2,128)(2,1)S(1)}, bf16[1,64,2,384]{3,2,1,0:T(2,128)(2,1)}, u32[]{:S(2)}) copy-start(bf16[1,64,2,384]{3,2,1,0:T(2,128)(2,1)} %param.19) | copy-start | bytes 294916
  7.2 114.0 %all-gather.5.cloned.1.call-start = ((), (), s32[]{:S(2)}) async-start(), calls=%async_computation.5 | async-start | bytes 2396160 | tf_op jit(solution)/shard_map/all_gather | solution.py:40
  7.9 252.3 %all-gather.7.cloned.1.call-start = ((), (), s32[]{:S(2)}) async-start(), calls=%async_computation.6 | async-start | bytes 2396160 | tf_op jit(solution)/shard_map/all_gather | solution.py:41
  13.4 25.9 %all-to-all-start = ((s32[64,1,3]{2,1,0:T(1,128)}), s32[64,1,3]{2,1,0:T(1,128)S(1)}, u32[]{:S(2)}, u32[]{:S(2)}) async-start(s32[64,1,3]{2,1,0:T(1,128)} %bitcast.4), calls=%async_computation | async-start | bytes 65536 | tf_op jit(solution)/shard_map/all_to_all | solution.py:185
  39.2 27.5 %all-to-all-start.1 = ((bf16[64,2,3072]{2,1,0:T(2,128)(2,1)}), bf16[64,2,3072]{2,1,0:T(2,128)(2,1)S(1)}, u32[]{:S(2)}, u32[]{:S(2)}) async-start(bf16[64,2,3072]{2,1,0:T(2,128)(2,1)} %gather_fusion.1), calls=%async_computation.1 | async-start | bytes 1572864 | tf_op jit(solution)/shard_map/all_to_all | solution.py:184
  70.5 13.4 %copy-start.5 = (s32[64]{0:T(128)S(1)}, s32[64]{0:T(128)}, u32[]{:S(2)}) copy-start(s32[64]{0:T(128)} %param.23) | copy-start | bytes 772
  70.5 15.1 %copy-start.3 = (f32[3072]{0:T(1024)S(1)}, f32[3072]{0:T(1024)}, u32[]{:S(2)}) copy-start(f32[3072]{0:T(1024)} %param.14) | copy-start | bytes 36868
  70.5 273.8 %all-to-all-start.2 = ((bf16[64,1,64,2,384]{4,2,3,1,0:T(8,128)(2,1)}), bf16[64,1,64,2,384]{4,2,3,1,0:T(8,128)(2,1)}, u32[]{:S(2)}, u32[]{:S(2)}) async-start(bf16[64,1,64,2,384]{4,2,3,1,0:T(8,128)(2,1)} %stack.13), calls=%async_computation.2 | async-start | bytes 12582912 | tf_op jit(solution)/shard_map/all_to_all | solution.py:108
  80.2 260.5 %all-gather.9.cloned.1.call-start = ((), (), s32[]{:S(2)}) async-start(), calls=%async_computation.7 | async-start | bytes 2396160 | tf_op jit(solution)/shard_map/all_gather | solution.py:42
  81.0 362.1 %all-gather.11.cloned.1.call-start = ((), (), s32[]{:S(2)}) async-start(), calls=%async_computation.8 | async-start | bytes 2396160 | tf_op jit(solution)/shard_map/all_gather | solution.py:196
  264.5 2.9 copy-start.1
  421.4 25.1 %copy-start.4 = (s32[64]{0:T(128)S(1)}, s32[64]{0:T(128)}, u32[]{:S(2)}) copy-start(s32[64]{0:T(128)} %param.20) | copy-start | bytes 772
  421.4 20.8 %all-to-all-start.3 = ((bf16[64,2,384]{2,1,0:T(2,128)(2,1)}), bf16[64,2,384]{2,1,0:T(2,128)(2,1)S(1)}, u32[]{:S(2)}, u32[]{:S(2)}) async-start(bf16[64,2,384]{2,1,0:T(2,128)(2,1)} %reshape.260), calls=%async_computation.3 | async-start | bytes 196608 | tf_op jit(solution)/shard_map/all_to_all | solution.py:192
  431.0 34.5 %reduce-scatter.2.cloned.1.call-start = ((), (), s32[]{:S(2)}) async-start(), calls=%async_computation.9 | async-start | bytes 983040 | tf_op jit(solution)/shard_map/reduce_scatter | solution.py:200
Sparse Core Ops, SparseCore 0:
  11.2 109.9 all-gather.4
  124.4 135.7 all-gather.6
  263.4 77.2 all-gather.8
  343.8 77.5 all-gather.10
  446.6 18.8 reduce-scatter.1
